TPU v7x, 128 devices: a whole 4x4x4 slice. The times are simulated.
128 devices in a mesh: lon: 32 (over y_hi, z, x), lat: 4 (over y_lo, core).
Axes of the slice: x: 4, y: 4 (y_hi: 2, y_lo: 2; y = y_hi * 2 + y_lo), z: 4, core: 2. Of those that a mesh axis runs over, the one named last changes fastest.
Arguments:
- state: float32 [25, 512, 4096], P(None, 'lat', 'lon'), may hold values from -6 to 6
- adjoint_in: float32 [25, 512, 4096], P(None, 'lat', 'lon'), may hold values from -6 to 6
- land_mask: int32 [512, 4096], P('lat', 'lon'), may hold values 0 or 1
- east_coef: float32 [512, 4096], P('lat', 'lon'), may hold values from 0.03 to 0.25
- north_coef: float32 [512, 4096], P('lat', 'lon'), may hold values from 0.03 to 0.25
- zonal_flow: float32 [512, 4096], P('lat', 'lon'), may hold values from -0.2 to 0.2
- vertical_coef: float32 [512, 4096], P('lat', 'lon'), may hold values from 0.05 to 0.3
- slot_cell: int32 [128, 8192], P(('lon', 'lat')), may hold values from -1 to 16383, as said below
- slot_weight: float32 [128, 8192], P(('lon', 'lat')), may hold values from 0.1 to 1
- arrive_obs: int32 [128, 8192], P(('lon', 'lat')), may hold values from -1 to 511, as said below
- obs_value: float32 [25, 65536], P(None, ('lon', 'lat')), may hold values from -6 to 6
- obs_invvar: float32 [25, 65536], P(None, ('lon', 'lat')), may hold values from 0.5 to 4
Outputs:
- adjoint_state: float32 [25, 512, 4096], P(None, 'lat', 'lon')
- misfit: float32 [25, 65536], P(None, ('lon', 'lat'))
Inputs may be any that keep to these rules, and one draw needn't show every extreme that they name: slot_cell[s, t * 64 + p] is the index, row-major over the 128 x 128 block of device s, of the cell that slot p from device s to device t reads, or -1 where that slot is empty; from each device to each device the live slots are those with p below a count of 1 to 64, and some device receives 64 live slots from every device. arrive_obs[t, s * 64 + p] is the observation of device t fed by slot p from device s, and is -1 exactly where slot_cell[s, t * 64 + p] is -1.
All inputs are finite; a program needn't handle non-finite values. No bound on the sum of `land_mask` on one device may be relied on, other than what follows from the above.
Results may differ from a plain program's by a relative error of at most 0.00002.
Values sent between devices are 32-bit elements; how exact they have to be, the bound alone decides.
A program may use at most 64 MiB of HBM per device.

v0:
```python
import jax
import jax.numpy as jnp
from jax import lax
from jax.experimental import pallas as pl
from jax.experimental.pallas import tpu as pltpu
from jax.sharding import PartitionSpec as P

BF = jnp.bfloat16
F32 = jnp.float32
I32 = jnp.int32
NW = 13
NT = (((1,), (1,)), ((), ()))


def iota(shape, dim):
    return lax.broadcasted_iota(I32, shape, dim)


def one_hot(rows, index):
    n = index.shape[1]
    return (iota((rows, n), 0) == index).astype(F32).astype(BF)


def cell_parts(cell):
    row = lax.bitwise_and(lax.shift_right_arithmetic(cell, 7), 63)
    half = lax.shift_left(lax.shift_right_arithmetic(cell, 13), 7)
    return row, lax.bitwise_or(half, lax.bitwise_and(cell, 127))


def remote(src, dst, send_sem, recv_sem, lon, lat):
    return pltpu.make_async_remote_copy(
        src_ref=src,
        dst_ref=dst,
        send_sem=send_sem,
        recv_sem=recv_sem,
        device_id={"lon": lon, "lat": lat},
        device_id_type=pl.DeviceIdType.MESH,
    )


def kernel(
    cell_ref, w_ref, obs_ref, state, adj, mask, east, north, zonal, vert, val, inv,
    out, mis,
    hi, lo, b0, b1, send, recv, acc, ms, back, ret, field, spread, mp, wst, est, wrv, erv,
    coef, ssem, rsem, bsem, tsem, nsem, nrem, hsem, hrem,
):
    a = lax.axis_index("lon")
    b = lax.axis_index("lat")
    me = a * 4 + b
    yhi = a // 16
    z = (a // 4) % 4
    x = a % 4

    def lon_at(j, sign):
        dx = j % 4
        dz = (j // 4 + j) % 4
        dy = (j // 16 + j) % 2
        return ((yhi + dy) % 2) * 16 + ((z + sign * dz + 4) % 4) * 4 + (x + sign * dx + 4) % 4

    def slot(ref, d):
        return ref.at[d, pl.ds(0, NW)]

    def put(src, dst, s1, s2, lon):
        def one(lat):
            remote(slot(src, lon * 4 + lat), slot(dst, me), s1, s2.at[me], lon, lat).start()

        for lat in range(4):
            if lon is a:
                pl.when(b != lat)(lambda: one(lat))
            else:
                one(lat)

    lane = iota((16, 128), 1)
    low = lane < 64
    live = iota((16, 128), 0) < NW

    def pack(va, vb):
        r = low[: va.shape[0]]
        return (
            jnp.where(r, va, pltpu.roll(vb, 64, 1)),
            jnp.where(r, pltpu.roll(va, 64, 1), vb),
        )

    def weights_at(o):
        cell = cell_ref[:, pl.ds(o, 256)]
        w = jnp.where(cell >= 0, w_ref[:, pl.ds(o, 256)], 0.0)
        row, col = cell_parts(cell)
        return w, row, col

    for half in range(2):
        v = state[:, half * 64 : half * 64 + 64, :].reshape(1600, 128)
        h = v.astype(BF)
        hi[:, half * 128 : half * 128 + 128] = h
        lo[:, half * 128 : half * 128 + 128] = (v - h.astype(F32)).astype(BF)

    def gather(lon):
        w, row, col = weights_at(pl.multiple_of(lon * 256, 256))
        cols = one_hot(256, col)
        rows = jnp.where(iota((64, 256), 0) == row, w, 0.0)
        for g in range(5):
            s = slice(g * 320, g * 320 + 320)
            t = jnp.dot(hi[s, :], cols, preferred_element_type=F32)
            t = t + jnp.dot(lo[s, :], cols, preferred_element_type=F32)
            t = t.reshape(5, 8, 8, 256) * rows.reshape(1, 8, 8, 256)
            t = jnp.sum(t, axis=1).reshape(40, 256)
            b0[pl.ds(g * 40, 40), :] = t[:, :128]
            b1[pl.ds(g * 40, 40), :] = t[:, 128:]

        def fold(ref, r0):
            y = ref[pl.ds(r0 * 8, NW, stride=8), :]
            for s in range(1, 8):
                y = y + ref[pl.ds(r0 * 8 + s, NW, stride=8), :]
            return y

        for q, ref in enumerate((b0, b1)):
            m0, m1 = pack(fold(ref, 0), fold(ref, NW))
            send[lon * 4 + 2 * q, 0:NW] = m0
            send[lon * 4 + 2 * q + 1, 0:NW] = m1

    def gather_step(j, _):
        gather(lon_at(j, 1))

        @pl.when(j > 1)
        def _():
            put(send, recv, ssem, rsem, lon_at(j - 1, 1))

        return 0

    lax.fori_loop(1, 32, gather_step, 0)
    gather(a)
    put(send, recv, ssem, rsem, lon_at(31, 1))
    recv[me, 0:NW] = send[me, 0:NW]
    put(send, recv, ssem, rsem, a)

    def take(src, dst, s1, s2, lon):
        def one(lat):
            remote(slot(src, lon * 4 + lat), slot(dst, lon * 4 + lat), s1, s2.at[lon * 4 + lat], lon, lat).wait_recv()

        for lat in range(4):
            if lon is a:
                pl.when(b != lat)(lambda: one(lat))
            else:
                one(lat)

    def unpack(ref, lon):
        xa = []
        xb = []
        for q in range(2):
            m0 = jnp.where(live, ref[lon * 4 + 2 * q], 0.0)
            m1 = jnp.where(live, ref[lon * 4 + 2 * q + 1], 0.0)
            va, vb = pack(m0, m1)
            xa.append(va)
            xb.append(vb)
        return jnp.concatenate(xa, 1), jnp.concatenate(xb, 1)

    acc[...] = jnp.zeros_like(acc)

    def observe(lon):
        ob = obs_ref[:, pl.ds(pl.multiple_of(lon * 256, 256), 256)]
        xx = jnp.concatenate(unpack(recv, lon), 0)
        h = xx.astype(BF).astype(F32)
        parts = jnp.concatenate([h, xx - h], 0).astype(BF)
        acc[...] += lax.dot_general(parts, one_hot(512, ob), NT, preferred_element_type=F32)

    def observe_step(j, _):
        lon = lon_at(j, -1)
        take(send, recv, ssem, rsem, lon)
        observe(lon)
        return 0

    lax.fori_loop(1, 32, observe_step, 0)
    take(send, recv, ssem, rsem, a)
    observe(a)
    ip = acc[0:32] + acc[32:64]
    ma = inv[0:13] * (ip[0:13] - val[0:13])
    mb = inv[13:25] * (ip[16:28] - val[13:25])
    mis[0:13] = ma
    mis[13:25] = mb
    ms[...] = jnp.zeros_like(ms)
    ms[0, 0:13] = ma
    ms[1, 0:12] = mb

    def answer(lon):
        for q in range(2):
            o = pl.multiple_of(lon * 256 + q * 128, 128)
            ob = jnp.maximum(obs_ref[:, pl.ds(o, 128)], 0)
            tile = jnp.broadcast_to(lax.shift_right_logical(ob, 7), (16, 128))
            at = jnp.broadcast_to(lax.bitwise_and(ob, 127), (16, 128))
            g = []
            for h in range(2):
                v = None
                for k in range(4):
                    u = jnp.take_along_axis(
                        ms[h, :, k * 128 : k * 128 + 128], at, axis=1, mode="promise_in_bounds"
                    )
                    v = u if v is None else jnp.where(tile == k, u, v)
                g.append(v)
            m0, m1 = pack(g[0], g[1])
            back[lon * 4 + 2 * q] = m0
            back[lon * 4 + 2 * q + 1] = m1

    def answer_step(j, _):
        answer(lon_at(j, 1))

        @pl.when(j > 1)
        def _():
            put(back, ret, bsem, tsem, lon_at(j - 1, 1))

        return 0

    lax.fori_loop(1, 32, answer_step, 0)
    answer(a)
    put(back, ret, bsem, tsem, lon_at(31, 1))
    ret[me] = back[me]
    put(back, ret, bsem, tsem, a)

    for half in range(2):
        field[:, half * 128 : half * 128 + 128] = adj[:, half * 64 : half * 64 + 64, :].reshape(1600, 128)

    def scatter(lon):
        w, row, col = weights_at(pl.multiple_of(lon * 256, 256))
        cols = one_hot(256, col)
        rows = one_hot(64, row)
        xa, xb = unpack(ret, lon)
        xa = xa * w
        xb = xb * w
        xah = xa.astype(BF).astype(F32)
        xbh = xb.astype(BF).astype(F32)
        for l in range(25):
            n = l if l < NW else l - NW
            for k, y in enumerate((xah, xa - xah) if l < NW else (xbh, xb - xbh)):
                spread[l * 64 : l * 64 + 64, k * 256 : k * 256 + 256] = (
                    rows * jnp.broadcast_to(y[n : n + 1], (64, 256)).astype(BF)
                )
        both = jnp.concatenate([cols, cols], 1)
        for g in range(5):
            s = slice(g * 320, g * 320 + 320)
            field[s, :] += lax.dot_general(spread[s, :], both, NT, preferred_element_type=F32)

    def scatter_step(j, _):
        lon = lon_at(j, -1)
        take(back, ret, bsem, tsem, lon)
        scatter(lon)
        return 0

    lax.fori_loop(1, 32, scatter_step, 0)
    take(back, ret, bsem, tsem, a)
    scatter(a)
    for half in range(2):
        out[:, half * 64 : half * 64 + 64, :] = field[:, half * 128 : half * 128 + 128].reshape(25, 64, 128)

    ocean = mask[...].astype(F32)
    own_e = east[...] + 0.5 * zonal[...]
    mp[0, 25, 8:136, :] = north[...]
    mp[0, 26, 8:136, :] = east[...] - 0.5 * zonal[...]
    last = b == 3

    @pl.when(b == 0)
    def _():
        mp[:, :, 7:8, :] = jnp.zeros((2, 27, 1, 128), F32)

    mirror = 127 - iota((32, 128), 1)
    wlane = iota((32, 128), 1)
    lane_r = iota((128, 128), 1)
    row_r = iota((128, 128), 0)
    w_lon = (a // 16) * 16 + a % 16
    west = (a + 31) % 32
    eastn = (a + 1) % 32

    for s in range(2):
        def stage(l, carry):
            wp, ep = carry
            m = mp[s, l, 8:136, :]
            for g in range(4):
                rows_g = m[g * 32 : g * 32 + 32]
                k = g * 32 + l
                wp = jnp.where(wlane == k, pltpu.roll(rows_g, (k + 1) % 128, 1), wp)
                ep = jnp.where(wlane == k, pltpu.roll(rows_g, k, 1), ep)
            return wp, ep

        def masked(l, _):
            mp[s, l, 8:136, :] = ocean * out[l]
            return 0

        lax.fori_loop(0, 25, masked, 0)
        n_lev = 27 if s == 0 else 25
        zero = jnp.zeros((32, 128), F32)
        wp, ep = lax.fori_loop(0, n_lev, stage, (zero, zero))
        wst[s] = wp
        est[s] = ep
        n_row = 26 if s == 0 else 25
        up = remote(mp.at[s, pl.ds(0, n_row), 135, :], mp.at[s, pl.ds(0, n_row), 7, :], nsem.at[s, 0], nrem.at[s, 0], a, b + 1)
        up_in = remote(mp.at[s, pl.ds(0, n_row), 135, :], mp.at[s, pl.ds(0, n_row), 7, :], nsem.at[s, 0], nrem.at[s, 0], a, b - 1)
        down = remote(mp.at[s, pl.ds(0, 25), 8, :], mp.at[s, pl.ds(0, 25), 136, :], nsem.at[s, 1], nrem.at[s, 1], a, b - 1)
        down_in = remote(mp.at[s, pl.ds(0, 25), 8, :], mp.at[s, pl.ds(0, 25), 136, :], nsem.at[s, 1], nrem.at[s, 1], a, b + 1)
        to_e = remote(wst.at[s], wrv.at[s], hsem.at[s, 0], hrem.at[s, 0], eastn, b)
        to_w = remote(est.at[s], erv.at[s], hsem.at[s, 1], hrem.at[s, 1], west, b)
        over = remote(coef.at[s, pl.ds(0, 25)], mp.at[s, pl.ds(0, 25), 136, :], nsem.at[s, 2], nrem.at[s, 2], 31 - a, b)

        @pl.when(last)
        def _():
            for l in range(25):
                coef[s, l : l + 1, :] = north[127:128, :] * mp[s, l, 135:136, :]
            coef[s] = jnp.take_along_axis(coef[s], mirror, axis=1, mode="promise_in_bounds")

        pl.when(b < 3)(lambda: up.start())
        pl.when(b > 0)(lambda: down.start())
        to_e.start()
        to_w.start()
        pl.when(last)(lambda: over.start())

        pl.when(b > 0)(lambda: up_in.wait_recv())
        pl.when(b < 3)(lambda: down_in.wait_recv())
        pl.when(last)(lambda: over.wait_recv())
        to_e.wait_recv()
        to_w.wait_recv()

        def west_of(l, m):
            return jnp.where(lane_r == 0, halo(wrv[s], l, 0), pltpu.roll(m, 1, 1))

        def east_of(l, m):
            return jnp.where(lane_r == 127, halo(erv[s], l, 1), pltpu.roll(m, 127, 1))

        def halo(h, l, shift):
            return jnp.concatenate(
                [pltpu.roll(h, (128 - shift - (g * 32 + l)) % 128, 1) for g in range(4)], 0
            )

        if s == 0:
            south_w = mp[0, 25, 7:135, :]
            west_w = west_of(26, mp[0, 26, 8:136, :])
            diag = own_e + west_w + north[...] + south_w
            north_w = jnp.where(jnp.logical_and(row_r == 127, last), 1.0, north[...])

        def step(l, _):
            m = mp[s, l, 8:136, :]
            above = jnp.where(l < 24, 1.0, 0.0)
            below = jnp.where(l > 0, 1.0, 0.0)
            v = out[l] - diag * m
            v = v + own_e * east_of(l, m) + west_w * west_of(l, m)
            v = v + north_w * mp[s, l, 9:137, :] + south_w * mp[s, l, 7:135, :]
            up_l = mp[s, jnp.minimum(l + 1, 24), 8:136, :]
            dn_l = mp[s, jnp.maximum(l - 1, 0), 8:136, :]
            v = v + vert[...] * (above * (up_l - m) + below * (dn_l - m))
            out[l] = v
            return 0

        lax.fori_loop(0, 25, step, 0)
        pl.when(b < 3)(lambda: up.wait_send())
        pl.when(b > 0)(lambda: down.wait_send())
        to_e.wait_send()
        to_w.wait_send()
        pl.when(last)(lambda: over.wait_send())

    many = pl.ds(0, 127)
    remote(send.at[many, pl.ds(0, NW)], recv.at[many, pl.ds(0, NW)], ssem, rsem.at[me], a, b).wait_send()
    remote(back.at[many, pl.ds(0, NW)], ret.at[many, pl.ds(0, NW)], bsem, tsem.at[me], a, b).wait_send()


def on_device(
    state, adjoint_in, land_mask, east_coef, north_coef, zonal_flow, vertical_coef,
    slot_cell, slot_weight, arrive_obs, obs_value, obs_invvar,
):
    dma = pltpu.SemaphoreType.DMA
    vm = pl.BlockSpec(memory_space=pltpu.VMEM)
    messages = pltpu.VMEM((128, 16, 128), F32)
    edge = pltpu.VMEM((2, 32, 128), F32)
    return pl.pallas_call(
        kernel,
        out_shape=(
            jax.ShapeDtypeStruct((25, 128, 128), F32),
            jax.ShapeDtypeStruct((25, 512), F32),
        ),
        in_specs=[vm] * 12,
        out_specs=(vm, vm),
        scratch_shapes=[
            pltpu.VMEM((1600, 256), BF),
            pltpu.VMEM((1600, 256), BF),
            pltpu.VMEM((208, 128), F32),
            pltpu.VMEM((208, 128), F32),
            messages,
            messages,
            pltpu.VMEM((64, 512), F32),
            pltpu.VMEM((2, 16, 512), F32),
            messages,
            messages,
            pltpu.VMEM((1600, 256), F32),
            pltpu.VMEM((1600, 512), BF),
            pltpu.VMEM((2, 27, 144, 128), F32),
            edge,
            edge,
            edge,
            edge,
            edge,
            dma,
            dma((128,)),
            dma,
            dma((128,)),
            dma((2, 3)),
            dma((2, 3)),
            dma((2, 2)),
            dma((2, 2)),
        ],
        compiler_params=pltpu.CompilerParams(vmem_limit_bytes=60 << 20, has_side_effects=True),
        name="adjoint",
    )(
        slot_cell, slot_weight, arrive_obs, state, adjoint_in, land_mask, east_coef, north_coef,
        zonal_flow, vertical_coef, obs_value, obs_invvar,
    )


def solution(mesh):
    grid = P("lat", "lon")
    cube = P(None, "lat", "lon")
    slots = P(("lon", "lat"), None)
    obs = P(None, ("lon", "lat"))
    return jax.shard_map(
        on_device,
        mesh=mesh,
        in_specs=(cube, cube, grid, grid, grid, grid, grid, slots, slots, slots, obs, obs),
        out_specs=(cube, obs),
        check_vma=False,
    )
```

profile of v0, /device:TPU:0, one launch (start us, length us, event | category | flops | bytes accessed | tf_op | source)
XLA Modules:
  0.0 107.8 jit_solution(309707722643207616)
XLA Ops:
  0.6 103.7 %adjoint.1 = (f32[25,128,128]{2,1,0:T(8,128)}, f32[25,512]{1,0:T(8,128)}) custom-call(s32[1,8192]{1,0:T(1,128)} %cell_ref.1, f32[1,8192]{1,0:T(1,128)} %w_ref.1, s32[1,8192]{1,0:T(1,128)} %obs_ref.1, f32[25,128,128]{2,1,0:T(8,128)} %state.1, f32[25,128,128]{2,1,0:T(8,128)} %adj.1, s32[128,128]{1,0:T(8,128)} %mask.1, f32[128,128]{1,0:T(8,128)} %east.1, ...), custom_call_target="tpu_custom_call" | custom-call | tf_op jit(solution)/shard_map/adjoint/pallas_call | solution.py:368
  104.4 0.0 copy-start
  104.4 2.8 %copy.16 = f32[25,128,128]{2,1,0:T(8,128)} copy(f32[25,128,128]{2,1,0:T(8,128)} %get-tuple-element.4) | data formatting | bytes 3276800
  107.2 0.0 copy-done
  107.2 0.6 copy.17
Async XLA Ops:
  104.4 2.8 %copy-start = (f32[25,512]{1,0:T(8,128)S(1)}, f32[25,512]{1,0:T(8,128)}, u32[]{:S(2)}) copy-start(f32[25,512]{1,0:T(8,128)} %get-tuple-element.5) | copy-start | bytes 153604
where the time goes:
time: 108 us
  Pallas kernels  104 us (96%)
  local copies, waits for them, and re-layouts  3.42 us (3%)
    pallas_call x1, Pallas kernels, on_device(): pl.pallas_call(kernel, out_shape=(jax.ShapeDtypeStruct((25, 128, 128), F3...  104 us
    unnamed x4, local copies, waits for them, and re-layouts  3.42 us

commit v1 on v0

--- a/solution.py
+++ b/solution.py
@@ -9,6 +9,7 @@
 F32 = jnp.float32
 I32 = jnp.int32
 NW = 13
+LEAD = 10
 NT = (((1,), (1,)), ((), ()))
 
 
@@ -39,23 +40,40 @@
 
 
 def kernel(
-    cell_ref, w_ref, obs_ref, state, adj, mask, east, north, zonal, vert, val, inv,
+    cell_ref, w_ref, obs_ref, state, adj_hbm, mask, east, north, zonal, vert, val, inv,
     out, mis,
-    hi, lo, b0, b1, send, recv, acc, ms, back, ret, field, spread, mp, wst, est, wrv, erv,
-    coef, ssem, rsem, bsem, tsem, nsem, nrem, hsem, hrem,
+    hi, lo, b0, b1, send, recv, acc, ms, back, ret, field, spread, mp, adj, u, cf, ed,
+    pp, ppw, ppe, rn, rs, nh, sh, fd, cst, crv, nst, nrv,
+    ssem, rsem, bsem, tsem, nsem, nrem, hsem, hrem, csem, crem, lsem,
 ):
     a = lax.axis_index("lon")
     b = lax.axis_index("lat")
     me = a * 4 + b
-    yhi = a // 16
-    z = (a // 4) % 4
-    x = a % 4
+    yhi = lax.div(a, 16)
+    z = lax.rem(lax.div(a, 4), 4)
+    x = lax.rem(a, 4)
 
     def lon_at(j, sign):
-        dx = j % 4
-        dz = (j // 4 + j) % 4
-        dy = (j // 16 + j) % 2
-        return ((yhi + dy) % 2) * 16 + ((z + sign * dz + 4) % 4) * 4 + (x + sign * dx + 4) % 4
+        dx = lax.rem(j, 4)
+        dz = lax.rem(lax.div(j, 4) + j, 4)
+        dy = lax.rem(lax.div(j, 16) + j + yhi, 2)
+        return dy * 16 + lax.rem(z + sign * dz + 4, 4) * 4 + lax.rem(x + sign * dx + 4, 4)
+
+    barrier = pltpu.get_barrier_semaphore()
+
+    def hello(t, _):
+        d = lax.rem(me + t, 128)
+        pl.semaphore_signal(
+            barrier,
+            inc=1,
+            device_id={"lon": lax.div(d, 4), "lat": lax.rem(d, 4)},
+            device_id_type=pl.DeviceIdType.MESH,
+        )
+        return 0
+
+    lax.fori_loop(1, 128, hello, 0)
+    load = pltpu.make_async_copy(adj_hbm, adj, lsem)
+    load.start()
 
     def slot(ref, d):
         return ref.at[d, pl.ds(0, NW)]
@@ -117,21 +135,6 @@
             send[lon * 4 + 2 * q, 0:NW] = m0
             send[lon * 4 + 2 * q + 1, 0:NW] = m1
 
-    def gather_step(j, _):
-        gather(lon_at(j, 1))
-
-        @pl.when(j > 1)
-        def _():
-            put(send, recv, ssem, rsem, lon_at(j - 1, 1))
-
-        return 0
-
-    lax.fori_loop(1, 32, gather_step, 0)
-    gather(a)
-    put(send, recv, ssem, rsem, lon_at(31, 1))
-    recv[me, 0:NW] = send[me, 0:NW]
-    put(send, recv, ssem, rsem, a)
-
     def take(src, dst, s1, s2, lon):
         def one(lat):
             remote(slot(src, lon * 4 + lat), slot(dst, lon * 4 + lat), s1, s2.at[lon * 4 + lat], lon, lat).wait_recv()
@@ -153,6 +156,33 @@
             xb.append(vb)
         return jnp.concatenate(xa, 1), jnp.concatenate(xb, 1)
 
+    last = b == 3
+    eastn = lax.rem(a + 1, 32)
+    westn = lax.rem(a + 31, 32)
+    lane_h = iota((64, 128), 1)
+    even = lax.rem(lane_h, 2) == 0
+    csend = remote(cst, crv, csem.at[0], crem.at[0], eastn, b)
+    nsend = remote(nst, nrv, csem.at[1], crem.at[1], a, b + 1)
+
+    def coefs_out():
+        csend.start()
+        pl.when(b < 3)(lambda: nsend.start())
+
+    weight = east[...] - 0.5 * zonal[...]
+    cst[...] = jnp.where(
+        lane_h < 64, pltpu.roll(weight[0:64], 1, 1), pltpu.roll(weight[64:128], 65, 1)
+    )
+    nst[...] = jnp.broadcast_to(north[127:128, :], (8, 128))
+
+    @pl.when(b == 0)
+    def _():
+        nrv[...] = jnp.zeros_like(nrv)
+        sh[...] = jnp.zeros_like(sh)
+
+    for s in range(2):
+        mp[s, pl.ds(7, 25, stride=144), :] = jnp.zeros((25, 128), F32)
+        mp[s, pl.ds(136, 25, stride=144), :] = jnp.zeros((25, 128), F32)
+
     acc[...] = jnp.zeros_like(acc)
 
     def observe(lon):
@@ -162,13 +192,41 @@
         parts = jnp.concatenate([h, xx - h], 0).astype(BF)
         acc[...] += lax.dot_general(parts, one_hot(512, ob), NT, preferred_element_type=F32)
 
+    def gather_only(j, _):
+        gather(lon_at(j, 1))
+        return 0
+
+    lax.fori_loop(1, LEAD + 1, gather_only, 0)
+    pl.semaphore_wait(barrier, 127)
+    coefs_out()
+
+    def burst(j, _):
+        put(send, recv, ssem, rsem, lon_at(j, 1))
+        return 0
+
+    lax.fori_loop(1, LEAD, burst, 0)
+
+    def gather_step(j, _):
+        put(send, recv, ssem, rsem, lon_at(j - 1, 1))
+        lon = lon_at(j - LEAD, -1)
+        take(send, recv, ssem, rsem, lon)
+        gather(lon_at(j, 1))
+        observe(lon)
+        return 0
+
+    lax.fori_loop(LEAD + 1, 32, gather_step, 0)
+    put(send, recv, ssem, rsem, lon_at(31, 1))
+    gather(a)
+    recv[me, 0:NW] = send[me, 0:NW]
+
     def observe_step(j, _):
         lon = lon_at(j, -1)
         take(send, recv, ssem, rsem, lon)
         observe(lon)
         return 0
 
-    lax.fori_loop(1, 32, observe_step, 0)
+    put(send, recv, ssem, rsem, a)
+    lax.fori_loop(32 - LEAD, 32, observe_step, 0)
     take(send, recv, ssem, rsem, a)
     observe(a)
     ip = acc[0:32] + acc[32:64]
@@ -199,20 +257,26 @@
             back[lon * 4 + 2 * q] = m0
             back[lon * 4 + 2 * q + 1] = m1
 
-    def answer_step(j, _):
-        answer(lon_at(j, 1))
-
-        @pl.when(j > 1)
-        def _():
-            put(back, ret, bsem, tsem, lon_at(j - 1, 1))
-
-        return 0
-
-    lax.fori_loop(1, 32, answer_step, 0)
+    answer(lon_at(1, 1))
+    answer(lon_at(2, 1))
+
+    def answer_step(i, _):
+        j = 2 * i
+        put(back, ret, bsem, tsem, lon_at(j - 1, 1))
+        put(back, ret, bsem, tsem, lon_at(j, 1))
+        answer(lon_at(j + 1, 1))
+        answer(lon_at(j + 2, 1))
+        return 0
+
+    lax.fori_loop(1, 15, answer_step, 0)
+    put(back, ret, bsem, tsem, lon_at(29, 1))
+    put(back, ret, bsem, tsem, lon_at(30, 1))
+    answer(lon_at(31, 1))
     answer(a)
     put(back, ret, bsem, tsem, lon_at(31, 1))
     ret[me] = back[me]
     put(back, ret, bsem, tsem, a)
+    load.wait()
 
     for half in range(2):
         field[:, half * 128 : half * 128 + 128] = adj[:, half * 64 : half * 64 + 64, :].reshape(1600, 128)
@@ -246,112 +310,112 @@
     lax.fori_loop(1, 32, scatter_step, 0)
     take(back, ret, bsem, tsem, a)
     scatter(a)
-    for half in range(2):
-        out[:, half * 64 : half * 64 + 64, :] = field[:, half * 128 : half * 128 + 128].reshape(25, 64, 128)
-
-    ocean = mask[...].astype(F32)
-    own_e = east[...] + 0.5 * zonal[...]
-    mp[0, 25, 8:136, :] = north[...]
-    mp[0, 26, 8:136, :] = east[...] - 0.5 * zonal[...]
-    last = b == 3
-
-    @pl.when(b == 0)
-    def _():
-        mp[:, :, 7:8, :] = jnp.zeros((2, 27, 1, 128), F32)
-
-    mirror = 127 - iota((32, 128), 1)
-    wlane = iota((32, 128), 1)
+    csend.wait_recv()
+    pl.when(b > 0)(lambda: nsend.wait_recv())
     lane_r = iota((128, 128), 1)
     row_r = iota((128, 128), 0)
-    w_lon = (a // 16) * 16 + a % 16
-    west = (a + 31) % 32
-    eastn = (a + 1) % 32
+    own_e = east[...] + 0.5 * zonal[...]
+    halo_w = jnp.concatenate([crv[...], pltpu.roll(crv[...], 64, 1)], 0)
+    west_w = jnp.where(lane_r == 0, halo_w, pltpu.roll(weight, 1, 1))
+    south_w = jnp.where(row_r == 0, nrv[0:1, :], pltpu.roll(north[...], 1, 0))
+    cf[0] = own_e + west_w + north[...] + south_w + 2.0 * vert[...]
+    cf[1] = jnp.where(lane_r == 127, 0.0, own_e)
+    cf[2] = jnp.where(lane_r == 0, 0.0, west_w)
+    cf[3] = south_w
+    cf[4] = mask[...].astype(F32)
+    south_0 = south_w[0:1, :]
+    north_127 = jnp.where(last, 1.0, north[127:128, :])
+    for g in range(2):
+        r = slice(g * 64, g * 64 + 64)
+        edge = jnp.where(
+            even,
+            jnp.broadcast_to(west_w[r, 0:1], (64, 128)),
+            jnp.broadcast_to(own_e[r, 127:128], (64, 128)),
+        )
+        cf[5, r, :] = edge
+    mirror = 127 - iota((25, 128), 1)
 
     for s in range(2):
-        def stage(l, carry):
-            wp, ep = carry
-            m = mp[s, l, 8:136, :]
-            for g in range(4):
-                rows_g = m[g * 32 : g * 32 + 32]
-                k = g * 32 + l
-                wp = jnp.where(wlane == k, pltpu.roll(rows_g, (k + 1) % 128, 1), wp)
-                ep = jnp.where(wlane == k, pltpu.roll(rows_g, k, 1), ep)
-            return wp, ep
-
-        def masked(l, _):
-            mp[s, l, 8:136, :] = ocean * out[l]
-            return 0
-
-        lax.fori_loop(0, 25, masked, 0)
-        n_lev = 27 if s == 0 else 25
-        zero = jnp.zeros((32, 128), F32)
-        wp, ep = lax.fori_loop(0, n_lev, stage, (zero, zero))
-        wst[s] = wp
-        est[s] = ep
-        n_row = 26 if s == 0 else 25
-        up = remote(mp.at[s, pl.ds(0, n_row), 135, :], mp.at[s, pl.ds(0, n_row), 7, :], nsem.at[s, 0], nrem.at[s, 0], a, b + 1)
-        up_in = remote(mp.at[s, pl.ds(0, n_row), 135, :], mp.at[s, pl.ds(0, n_row), 7, :], nsem.at[s, 0], nrem.at[s, 0], a, b - 1)
-        down = remote(mp.at[s, pl.ds(0, 25), 8, :], mp.at[s, pl.ds(0, 25), 136, :], nsem.at[s, 1], nrem.at[s, 1], a, b - 1)
-        down_in = remote(mp.at[s, pl.ds(0, 25), 8, :], mp.at[s, pl.ds(0, 25), 136, :], nsem.at[s, 1], nrem.at[s, 1], a, b + 1)
-        to_e = remote(wst.at[s], wrv.at[s], hsem.at[s, 0], hrem.at[s, 0], eastn, b)
-        to_w = remote(est.at[s], erv.at[s], hsem.at[s, 1], hrem.at[s, 1], west, b)
-        over = remote(coef.at[s, pl.ds(0, 25)], mp.at[s, pl.ds(0, 25), 136, :], nsem.at[s, 2], nrem.at[s, 2], 31 - a, b)
-
-        @pl.when(last)
-        def _():
-            for l in range(25):
-                coef[s, l : l + 1, :] = north[127:128, :] * mp[s, l, 135:136, :]
-            coef[s] = jnp.take_along_axis(coef[s], mirror, axis=1, mode="promise_in_bounds")
-
-        pl.when(b < 3)(lambda: up.start())
-        pl.when(b > 0)(lambda: down.start())
+        to_n = remote(rn.at[s], sh.at[s], nsem.at[s, 0], nrem.at[s, 0], a, b + 1)
+        to_s = remote(rs.at[s], nh.at[s], nsem.at[s, 1], nrem.at[s, 1], a, b - 1)
+        over = remote(fd.at[s], nh.at[s], nsem.at[s, 2], nrem.at[s, 2], 31 - a, b)
+        to_e = remote(pp.at[s], ppw.at[s], hsem.at[s, 0], hrem.at[s, 0], eastn, b)
+        to_w = remote(pp.at[s], ppe.at[s], hsem.at[s, 1], hrem.at[s, 1], westn, b)
+        packed = [jnp.zeros((64, 128), F32)] * 2
+        for l in range(25):
+            if s == 0:
+                v = jnp.concatenate(
+                    [field[l * 64 : l * 64 + 64, 0:128], field[l * 64 : l * 64 + 64, 128:256]], 0
+                )
+            else:
+                v = u[l * 128 : l * 128 + 128, :] + edges(0, l)
+            u[l * 128 : l * 128 + 128, :] = v
+            m = cf[4] * v
+            mp[s, l * 144 + 8 : l * 144 + 136, :] = m
+            for g in range(2):
+                k = g * 64 + 2 * l
+                sel = (lane_h == k) | (lane_h == (k + 127) % 128)
+                packed[g] = jnp.where(sel, pltpu.roll(m[g * 64 : g * 64 + 64], k, 1), packed[g])
+        top = mp[s, pl.ds(135, 25, stride=144), :]
+        rn[s, 0:25] = top
+        rs[s, 0:25] = mp[s, pl.ds(8, 25, stride=144), :]
+        fd[s, 0:25] = jnp.take_along_axis(
+            north[127:128, :] * top, mirror, axis=1, mode="promise_in_bounds"
+        )
+        pp[s] = jnp.where(lane_h == 127, packed[0], jnp.where(lane_h < 63, packed[0], packed[1]))
+
+        pl.when(b < 3)(lambda: to_n.start())
+        pl.when(b > 0)(lambda: to_s.start())
+        pl.when(last)(lambda: over.start())
         to_e.start()
         to_w.start()
-        pl.when(last)(lambda: over.start())
-
-        pl.when(b > 0)(lambda: up_in.wait_recv())
-        pl.when(b < 3)(lambda: down_in.wait_recv())
+
+        def step(l, _):
+            base = pl.multiple_of(l * 144, 8)
+            m = mp[s, pl.ds(base + 8, 128), :]
+            at = pl.ds(pl.multiple_of(l * 128, 8), 128)
+            v = u[at, :] - cf[0] * m
+            v = v + cf[1] * pltpu.roll(m, 127, 1) + cf[2] * pltpu.roll(m, 1, 1)
+            v = v + north[...] * mp[s, pl.ds(base + 9, 128), :]
+            v = v + cf[3] * mp[s, pl.ds(base + 7, 128), :]
+            hi_l = pl.multiple_of(jnp.minimum(l + 1, 24) * 144, 8)
+            lo_l = pl.multiple_of(jnp.maximum(l - 1, 0) * 144, 8)
+            v = v + vert[...] * (mp[s, pl.ds(hi_l + 8, 128), :] + mp[s, pl.ds(lo_l + 8, 128), :])
+            u[at, :] = v
+            return 0
+
+        lax.fori_loop(0, 25, step, 0)
+        pl.when(b > 0)(lambda: to_n.wait_recv())
+        pl.when(b < 3)(lambda: to_s.wait_recv())
         pl.when(last)(lambda: over.wait_recv())
         to_e.wait_recv()
         to_w.wait_recv()
-
-        def west_of(l, m):
-            return jnp.where(lane_r == 0, halo(wrv[s], l, 0), pltpu.roll(m, 1, 1))
-
-        def east_of(l, m):
-            return jnp.where(lane_r == 127, halo(erv[s], l, 1), pltpu.roll(m, 127, 1))
-
-        def halo(h, l, shift):
-            return jnp.concatenate(
-                [pltpu.roll(h, (128 - shift - (g * 32 + l)) % 128, 1) for g in range(4)], 0
+        u[pl.ds(127, 25, stride=128), :] += north_127 * nh[s, 0:25]
+        u[pl.ds(0, 25, stride=128), :] += south_0 * sh[s, 0:25]
+        wide = jnp.where(even, pltpu.roll(ppw[s], 1, 1), pltpu.roll(ppe[s], 127, 1))
+        ed[s, 0:64, :] = wide * cf[5, 0:64, :]
+        ed[s, 64:128, :] = wide * cf[5, 64:128, :]
+
+        def edges(s, l):
+            y = jnp.concatenate(
+                [
+                    pltpu.roll(ed[s, g * 64 : g * 64 + 64, :], (128 - g * 64 - 2 * l) % 128, 1)
+                    for g in range(2)
+                ],
+                0,
             )
-
-        if s == 0:
-            south_w = mp[0, 25, 7:135, :]
-            west_w = west_of(26, mp[0, 26, 8:136, :])
-            diag = own_e + west_w + north[...] + south_w
-            north_w = jnp.where(jnp.logical_and(row_r == 127, last), 1.0, north[...])
-
-        def step(l, _):
-            m = mp[s, l, 8:136, :]
-            above = jnp.where(l < 24, 1.0, 0.0)
-            below = jnp.where(l > 0, 1.0, 0.0)
-            v = out[l] - diag * m
-            v = v + own_e * east_of(l, m) + west_w * west_of(l, m)
-            v = v + north_w * mp[s, l, 9:137, :] + south_w * mp[s, l, 7:135, :]
-            up_l = mp[s, jnp.minimum(l + 1, 24), 8:136, :]
-            dn_l = mp[s, jnp.maximum(l - 1, 0), 8:136, :]
-            v = v + vert[...] * (above * (up_l - m) + below * (dn_l - m))
-            out[l] = v
-            return 0
-
-        lax.fori_loop(0, 25, step, 0)
-        pl.when(b < 3)(lambda: up.wait_send())
-        pl.when(b > 0)(lambda: down.wait_send())
+            return jnp.where((lane_r == 0) | (lane_r == 127), y, 0.0)
+
+        pl.when(b < 3)(lambda: to_n.wait_send())
+        pl.when(b > 0)(lambda: to_s.wait_send())
+        pl.when(last)(lambda: over.wait_send())
         to_e.wait_send()
         to_w.wait_send()
-        pl.when(last)(lambda: over.wait_send())
-
+
+    for l in range(25):
+        out[l] = u[l * 128 : l * 128 + 128, :] + edges(1, l)
+    csend.wait_send()
+    pl.when(b < 3)(lambda: nsend.wait_send())
     many = pl.ds(0, 127)
     remote(send.at[many, pl.ds(0, NW)], recv.at[many, pl.ds(0, NW)], ssem, rsem.at[me], a, b).wait_send()
     remote(back.at[many, pl.ds(0, NW)], ret.at[many, pl.ds(0, NW)], bsem, tsem.at[me], a, b).wait_send()
@@ -364,14 +428,15 @@
     dma = pltpu.SemaphoreType.DMA
     vm = pl.BlockSpec(memory_space=pltpu.VMEM)
     messages = pltpu.VMEM((128, 16, 128), F32)
-    edge = pltpu.VMEM((2, 32, 128), F32)
+    columns = pltpu.VMEM((2, 64, 128), F32)
+    rows = pltpu.VMEM((2, 32, 128), F32)
     return pl.pallas_call(
         kernel,
         out_shape=(
             jax.ShapeDtypeStruct((25, 128, 128), F32),
             jax.ShapeDtypeStruct((25, 512), F32),
         ),
-        in_specs=[vm] * 12,
+        in_specs=[vm] * 4 + [pl.BlockSpec(memory_space=pl.ANY)] + [vm] * 7,
         out_specs=(vm, vm),
         scratch_shapes=[
             pltpu.VMEM((1600, 256), BF),
@@ -386,12 +451,23 @@
             messages,
             pltpu.VMEM((1600, 256), F32),
             pltpu.VMEM((1600, 512), BF),
-            pltpu.VMEM((2, 27, 144, 128), F32),
-            edge,
-            edge,
-            edge,
-            edge,
-            edge,
+            pltpu.VMEM((2, 3600, 128), F32),
+            pltpu.VMEM((25, 128, 128), F32),
+            pltpu.VMEM((3200, 128), F32),
+            pltpu.VMEM((6, 128, 128), F32),
+            pltpu.VMEM((2, 128, 128), F32),
+            columns,
+            columns,
+            columns,
+            rows,
+            rows,
+            rows,
+            rows,
+            rows,
+            pltpu.VMEM((64, 128), F32),
+            pltpu.VMEM((64, 128), F32),
+            pltpu.VMEM((8, 128), F32),
+            pltpu.VMEM((8, 128), F32),
             dma,
             dma((128,)),
             dma,
@@ -400,8 +476,11 @@
             dma((2, 3)),
             dma((2, 2)),
             dma((2, 2)),
+            dma((2,)),
+            dma((2,)),
+            dma,
         ],
-        compiler_params=pltpu.CompilerParams(vmem_limit_bytes=60 << 20, has_side_effects=True),
+        compiler_params=pltpu.CompilerParams(vmem_limit_bytes=60 << 20, has_side_effects=True, collective_id=0),
         name="adjoint",
     )(
         slot_cell, slot_weight, arrive_obs, state, adjoint_in, land_mask, east_coef, north_coef,

time: 108 us -> 94.8 us (0.88)
  Pallas kernels: 104 us -> 90.5 us
    pallas_call x1, Pallas kernels: 104 us -> 90.5 us  [on_device(): pl.pallas_call(kernel, out_shape=(jax.ShapeDtypeStruct((25, 128, 128), F3...]
where the time goes in v1:
time: 94.8 us; the launch traced here: 94.6 us
  Pallas kernels  90.5 us (95%)
  local copies, waits for them, and re-layouts  3.42 us (4%)
    pallas_call x1, Pallas kernels, on_device(): pl.pallas_call(kernel, out_shape=(jax.ShapeDtypeStruct((25, 128, 128), F3...  90.5 us
    unnamed x4, local copies, waits for them, and re-layouts  3.42 us

profile of v1, /device:TPU:0, one launch (start us, length us, event | category | flops | bytes accessed | tf_op | source)
XLA Modules:
  0.0 94.6 jit_solution(3373493706861348640)
XLA Ops:
  0.6 90.5 %adjoint.1 = (f32[25,128,128]{2,1,0:T(8,128)}, f32[25,512]{1,0:T(8,128)}) custom-call(s32[1,8192]{1,0:T(1,128)} %cell_ref.1, f32[1,8192]{1,0:T(1,128)} %w_ref.1, s32[1,8192]{1,0:T(1,128)} %obs_ref.1, f32[25,128,128]{2,1,0:T(8,128)} %state.1, f32[25,128,128]{2,1,0:T(8,128)} %adj_hbm.1, s32[128,128]{1,0:T(8,128)} %mask.1, f32[128,128]{1,0:T(8,128)} %east.1, ...), custom_call_target="tpu_custom_call" | custom-call | tf_op jit(solution)/shard_map/adjoint/pallas_call | solution.py:433
  91.1 0.0 copy-start
  91.1 2.8 %copy.16 = f32[25,128,128]{2,1,0:T(8,128)} copy(f32[25,128,128]{2,1,0:T(8,128)} %get-tuple-element.4) | data formatting | bytes 3276800
  93.9 0.0 copy-done
  93.9 0.6 copy.17
Async XLA Ops:
  91.1 2.8 %copy-start = (f32[25,512]{1,0:T(8,128)S(1)}, f32[25,512]{1,0:T(8,128)}, u32[]{:S(2)}) copy-start(f32[25,512]{1,0:T(8,128)} %get-tuple-element.5) | copy-start | bytes 153604
